TPU v7x, 256 devices: a whole 4x4x8 slice. The times are simulated.
256 devices in a mesh: fsdp: 8 (over x_hi, y), ctx: 32 (over z, x_lo, core).
Axes of the slice: x: 4 (x_hi: 2, x_lo: 2; x = x_hi * 2 + x_lo), y: 4, z: 8, core: 2. Of those that a mesh axis runs over, the one named last changes fastest.
Arguments:
- tokens: bfloat16 [8, 4096, 1024], P('fsdp', 'ctx'), may hold values from -16 to 16
- cotangent: bfloat16 [8, 4096, 1024], P('fsdp', 'ctx'), may hold values from -6 to 6
- w_query: bfloat16 [1024, 512], P('fsdp')
- w_key: bfloat16 [1024, 512], P('fsdp')
- w_value: bfloat16 [1024, 512], P('fsdp'), may hold values from -0.1875 to 0.1875
- w_out: bfloat16 [512, 1024], P('fsdp'), may hold values from -0.25 to 0.25
- block_mask: int32 [32, 32], replicated, may hold values from 0 to 1, as said below
- span_order: int32 [64], replicated, may hold values from 0 to 63, each once
Outputs:
- mixed_out: bfloat16 [8, 4096, 1024], P('fsdp', 'ctx')
- token_grad: bfloat16 [8, 4096, 1024], P('fsdp', 'ctx')
- grad_query: float32 [1024, 512], P(('fsdp', 'ctx'))
- grad_key: float32 [1024, 512], P(('fsdp', 'ctx'))
- grad_value: float32 [1024, 512], P(('fsdp', 'ctx'))
- grad_out: float32 [512, 1024], P(('fsdp', 'ctx'))
Inputs may be any that keep to these rules, and one draw needn't show every extreme that they name: `block_mask`: every diagonal entry is 1.
All inputs are finite; a program needn't handle non-finite values.
Results may differ from a plain program's by a relative error of at most 0.013.
The roundings to bfloat16 on the way count: a program that leaves them out, or rounds other values in their place, can miss the bound.
Values may be sent and summed in bfloat16 or wider, within the bound.
No kernel may reach another device: no remote copies, remote signals or barrier semaphores. Data moves between devices by JAX's collectives and lax.ppermute only.
A program may use at most 128 MiB of HBM per device.

v0:
```python
import math
import jax
import jax.numpy as jnp
from jax import lax
from jax.sharding import PartitionSpec as P

HEADS = 4
HD = 128
BLK = 128
SPAN = 64
NEG = -1e30
HIGH = lax.Precision.HIGHEST


def block_ids(span_order, start, count):
    rows = start + jnp.arange(count, dtype=jnp.int32)
    span = rows // SPAN
    lanes = jnp.arange(span_order.shape[0], dtype=jnp.int32)
    first = jnp.sum(jnp.where(span[:, None] == lanes[None, :], span_order[None, :], 0), axis=1)
    return (first * SPAN + rows % SPAN) // BLK


def allowed_between(mask_f, row_ids, col_ids):
    lanes = jnp.arange(mask_f.shape[0], dtype=jnp.int32)
    left = (row_ids[:, None] == lanes[None, :]).astype(jnp.float32)
    right = (col_ids[:, None] == lanes[None, :]).astype(jnp.float32)
    linked = jnp.dot(jnp.dot(left, mask_f), right.T)
    return linked > 0.5


def over_blocks(step, carry, pieces):
    count = pieces[0].shape[0]
    width = 512
    stacked = tuple((piece.reshape((count // width, width) + piece.shape[1:]) for piece in pieces))

    def scan_step(state, item):
        number, parts = item
        return (step(state, parts, number * width), None)

    numbers = jnp.arange(count // width, dtype=jnp.int32)
    carry, _ = lax.scan(scan_step, carry, (numbers, stacked))
    return carry


def contract_rows(left, right):
    return lax.dot_general(
        left, right, (((0,), (0,)), ((), ())), preferred_element_type=jnp.float32
    )


def contract_cols(left, right):
    return lax.dot_general(
        left, right, (((1,), (1,)), ((), ())), preferred_element_type=jnp.float32
    )


def body(tokens, cotangent, w_query, w_key, w_value, w_out, block_mask, span_order):
    x_rows = tokens[0]
    dy_rows = cotangent[0]
    rows = x_rows.shape[0]
    scale = 1.0 / math.sqrt(HD)
    full_q, full_k, full_v, full_o = (
        lax.all_gather(w_query, "fsdp", axis=0, tiled=True),
        lax.all_gather(w_key, "fsdp", axis=0, tiled=True),
        lax.all_gather(w_value, "fsdp", axis=0, tiled=True),
        lax.all_gather(w_out, "fsdp", axis=0, tiled=True),
    )
    query = jnp.dot(x_rows, full_q, preferred_element_type=jnp.float32).astype(jnp.bfloat16)
    keys = jnp.dot(x_rows, full_k, preferred_element_type=jnp.float32).astype(jnp.bfloat16)
    values = jnp.dot(x_rows, full_v, preferred_element_type=jnp.float32).astype(jnp.bfloat16)
    d_attn = contract_cols(dy_rows, full_o).astype(jnp.bfloat16)
    mask_f = block_mask.astype(jnp.float32)
    own_ids = block_ids(span_order, lax.axis_index("ctx") * rows, rows)
    q_own = query.reshape(rows, HEADS, HD)
    k_own = keys.reshape(rows, HEADS, HD)
    v_own = values.reshape(rows, HEADS, HD)
    g_own = d_attn.reshape(rows, HEADS, HD)

    def sweep_keys(carry, parts, start):
        top, total, out_acc, mix_acc, key_acc, dot_acc = carry
        count = parts[0].shape[0]
        k_part = parts[0].reshape(count, HEADS, HD)
        v_part = parts[1].reshape(count, HEADS, HD)
        keep = allowed_between(mask_f, own_ids, block_ids(span_order, start, count))[None]
        score = (
            jnp.einsum("qhd,khd->hqk", q_own, k_part, preferred_element_type=jnp.float32) * scale
        )
        score = jnp.where(keep, score, NEG)
        new_top = jnp.maximum(top, jnp.max(score, axis=-1))
        fade = jnp.exp(top - new_top)
        prob = jnp.where(keep, jnp.exp(score - new_top[:, :, None]), 0.0)
        k_wide = k_part.astype(jnp.float32)
        v_wide = v_part.astype(jnp.float32)
        total = fade * total + jnp.sum(prob, axis=-1)
        out_acc = fade[:, :, None] * out_acc + jnp.einsum(
            "hqk,khd->hqd", prob, v_wide, precision=HIGH
        )
        d_prob = jnp.einsum("qhd,khd->hqk", g_own, v_part, preferred_element_type=jnp.float32)
        weighted = prob * d_prob
        dot_acc = fade * dot_acc + jnp.sum(weighted, axis=-1)
        mix_acc = fade[:, :, None] * mix_acc + jnp.einsum(
            "hqk,khd->hqd", weighted, k_wide, precision=HIGH
        )
        key_acc = fade[:, :, None] * key_acc + jnp.einsum(
            "hqk,khd->hqd", prob, k_wide, precision=HIGH
        )
        return (new_top, total, out_acc, mix_acc, key_acc, dot_acc)

    flat = jnp.zeros((HEADS, rows), jnp.float32)
    cube = jnp.zeros((HEADS, rows, HD), jnp.float32)
    begin = (jnp.full((HEADS, rows), NEG, jnp.float32), flat, cube, cube, cube, flat)
    top, total, out_acc, mix_acc, key_acc, dot_acc = over_blocks(
        sweep_keys,
        begin,
        (
            lax.all_gather(keys, "ctx", axis=0, tiled=True),
            lax.all_gather(values, "ctx", axis=0, tiled=True),
        ),
    )
    share = 1.0 / total
    combined = out_acc * share[:, :, None]
    log_total = top + jnp.log(total)
    attention = jnp.transpose(combined, (1, 0, 2)).reshape(rows, HEADS * HD).astype(jnp.bfloat16)
    mixed = (
        x_rows.astype(jnp.float32) + jnp.dot(attention, full_o, preferred_element_type=jnp.float32)
    ).astype(jnp.bfloat16)
    delta = dot_acc * share
    log_rows = jnp.transpose(log_total)
    delta_rows = jnp.transpose(delta)

    def key_side(acc, parts, start):
        d_key, d_value = acc
        count = parts[0].shape[0]
        q_part = parts[0].reshape(count, HEADS, HD)
        g_part = parts[1].reshape(count, HEADS, HD)
        lse_part = jnp.transpose(parts[2])
        delta_part = jnp.transpose(parts[3])
        keep = allowed_between(mask_f, block_ids(span_order, start, count), own_ids)[None]
        score = (
            jnp.einsum("khd,qhd->hkq", q_part, k_own, preferred_element_type=jnp.float32) * scale
        )
        score = jnp.where(keep, score, NEG)
        prob = jnp.where(keep, jnp.exp(score - lse_part[:, :, None]), 0.0)
        d_prob = jnp.einsum("khd,qhd->hkq", g_part, v_own, preferred_element_type=jnp.float32)
        d_score = prob * (d_prob - delta_part[:, :, None])
        d_key = d_key + scale * jnp.einsum(
            "hkq,khd->hqd", d_score, q_part.astype(jnp.float32), precision=HIGH
        )
        d_value = d_value + jnp.einsum(
            "hkq,khd->hqd", prob, g_part.astype(jnp.float32), precision=HIGH
        )
        return (d_key, d_value)

    d_query = scale * (mix_acc - delta[:, :, None] * key_acc) * share[:, :, None]
    d_key, d_value = over_blocks(
        key_side,
        (cube, cube),
        (
            lax.all_gather(query.astype(jnp.float32), "ctx", axis=0, tiled=True).astype(
                jnp.bfloat16
            ),
            lax.all_gather(d_attn.astype(jnp.float32), "ctx", axis=0, tiled=True).astype(
                jnp.bfloat16
            ),
            lax.all_gather(log_rows, "ctx", axis=0, tiled=True),
            lax.all_gather(delta_rows, "ctx", axis=0, tiled=True),
        ),
    )

    def to_rows(grad_heads):
        return jnp.transpose(grad_heads, (1, 0, 2)).reshape(rows, HEADS * HD).astype(jnp.bfloat16)

    dq_rows = to_rows(d_query)
    dk_rows = to_rows(d_key)
    dv_rows = to_rows(d_value)
    token_grad = (
        dy_rows.astype(jnp.float32)
        + contract_cols(dq_rows, full_q)
        + contract_cols(dk_rows, full_k)
        + contract_cols(dv_rows, full_v)
    ).astype(jnp.bfloat16)
    grad_q = contract_rows(x_rows, dq_rows)
    grad_k = contract_rows(x_rows, dk_rows)
    grad_v = contract_rows(x_rows, dv_rows)
    grad_o = contract_rows(attention, dy_rows)
    grad_q, grad_k, grad_v, grad_o = (
        lax.psum_scatter(grad_q, ("fsdp", "ctx"), scatter_dimension=0, tiled=True),
        lax.psum_scatter(grad_k, ("fsdp", "ctx"), scatter_dimension=0, tiled=True),
        lax.psum_scatter(grad_v, ("fsdp", "ctx"), scatter_dimension=0, tiled=True),
        lax.psum_scatter(grad_o, ("fsdp", "ctx"), scatter_dimension=0, tiled=True),
    )
    return (mixed[None], token_grad[None], grad_q, grad_k, grad_v, grad_o)


def solution(mesh):
    return jax.shard_map(
        body,
        mesh=mesh,
        in_specs=(
            P("fsdp", "ctx", None),
            P("fsdp", "ctx", None),
            P("fsdp", None),
            P("fsdp", None),
            P("fsdp", None),
            P("fsdp", None),
            P(),
            P(),
        ),
        out_specs=(
            P("fsdp", "ctx", None),
            P("fsdp", "ctx", None),
            P(("fsdp", "ctx"), None),
            P(("fsdp", "ctx"), None),
            P(("fsdp", "ctx"), None),
            P(("fsdp", "ctx"), None),
        ),
        check_vma=False,
    )
```

profile of v0, /device:TPU:2, one launch (start us, length us, event | category | flops | bytes accessed | tf_op | source)
XLA Modules:
  0.0 907.5 jit_solution(11538158528910636079)
XLA Ops:
  10.0 54.1 %all-gather.9.cloned.1.call-done = bf16[1024,512]{1,0:T(8,128)(2,1)} async-done(((bf16[128,512]{1,0:T(8,128)(2,1)}), bf16[1024,512]{1,0:T(8,128)(2,1)}) %all-gather.9.cloned.1.call-update) | async-done | bytes 1048592 | tf_op jit(solution)/shard_map/all_gather | solution.py:64
  64.1 2.3 convolution_convert_fusion.3
  66.5 50.6 %all-gather.15.cloned.1.call-done = bf16[1024,512]{1,0:T(8,128)(2,1)} async-done(((bf16[128,512]{1,0:T(8,128)(2,1)}), bf16[1024,512]{1,0:T(8,128)(2,1)}) %all-gather.15.cloned.1.call-update) | async-done | bytes 1048592 | tf_op jit(solution)/shard_map/all_gather | solution.py:65
  117.1 2.2 convolution_convert_fusion.1
  119.3 50.7 %all-gather.13.cloned.1.call-done = bf16[1024,512]{1,0:T(8,128)(2,1)} async-done(((bf16[128,512]{1,0:T(8,128)(2,1)}), bf16[1024,512]{1,0:T(8,128)(2,1)}) %all-gather.13.cloned.1.call-update) | async-done | bytes 1048592 | tf_op jit(solution)/shard_map/all_gather | solution.py:63
  170.0 2.2 convolution_convert_fusion.2
  175.9 46.9 %all-gather.19.cloned.1.call-done = bf16[512,1024]{1,0:T(8,128)(2,1)} async-done(((bf16[64,1024]{1,0:T(8,128)(2,1)}), bf16[512,1024]{1,0:T(8,128)(2,1)}) %all-gather.19.cloned.1.call-update) | async-done | bytes 1048592 | tf_op jit(solution)/shard_map/all_gather | solution.py:66
  222.8 1.7 convolution_convert_fusion
  225.2 65.8 %all-gather.11.cloned.1.call-done = bf16[4096,512]{1,0:T(8,128)(2,1)} async-done(((bf16[128,512]{1,0:T(8,128)(2,1)}), bf16[4096,512]{1,0:T(8,128)(2,1)}) %all-gather.11.cloned.1.call-update) | async-done | bytes 4194320 | tf_op jit(solution)/shard_map/all_gather | solution.py:116
  291.1 68.8 %all-gather.17.cloned.1.call-done = bf16[4096,512]{1,0:T(8,128)(2,1)} async-done(((bf16[128,512]{1,0:T(8,128)(2,1)}), bf16[4096,512]{1,0:T(8,128)(2,1)}) %all-gather.17.cloned.1.call-update) | async-done | bytes 4194320 | tf_op jit(solution)/shard_map/all_gather | solution.py:117
  360.4 75.2 %while.40 = (s32[]{:T(128)}, f32[4,128]{1,0:T(4,128)S(1)}, f32[4,128]{1,0:T(4,128)S(1)}, f32[4,128,128]{2,1,0:T(8,128)S(1)}, f32[4,128,128]{2,1,0:T(8,128)S(1)},...) while((s32[]{:T(128)}, f32[4,128]{1,0:T(4,128)S(1)}, ...), condition=%wide.region_6.7_spmd.clone, body=%wide.region_1.6_spmd.clone.sunk | while | flops 1351104000 | bytes 16581600 | solution.py:41
  397.9 1.3 constant_dynamic-slice_fusion.10
  416.7 1.3 constant_dynamic-slice_fusion.10
  438.1 34.6 %all_gather.37 = f32[4096,4]{0,1:T(4,128)} all-gather(f32[128,4]{0,1:T(4,128)S(1)} %get-tuple-element.758), channel_id=1, replica_groups=mesh['fsdp'=8,'ctx'=32] {'ctx'}, dimensions={0}, use_global_device_ids=true | all-gather | bytes 67584 | tf_op jit(solution)/shard_map/all_gather | solution.py:165
  472.7 33.9 %all_gather.39 = f32[4096,4]{0,1:T(4,128)} all-gather(f32[128,4]{0,1:T(4,128)S(1)} %bitcast.204), channel_id=1, replica_groups=mesh['fsdp'=8,'ctx'=32] {'ctx'}, dimensions={0}, use_global_device_ids=true | all-gather | bytes 67584 | tf_op jit(solution)/shard_map/all_gather | solution.py:166
  507.2 97.2 %while.41 = (s32[]{:T(128)}, f32[4,128,128]{2,1,0:T(8,128)}, f32[4,128,128]{2,1,0:T(8,128)}, s32[8]{0:T(128)}, s32[64]{0:T(128)S(1)}, /*index=5*/bf16[32,32]{1,0...) while((s32[]{:T(128)}, f32[4,128,128]{2,1,0:T(8,128)}, ...), condition=%wide.region_9.10_spmd.clone, body=%wide.region_7.9_spmd.clone.sunk | while | flops 946874368 | bytes 14089224 | solution.py:41
  507.2 1.3 constant_dynamic-slice_fusion.11
  514.2 1.8 fusion.146
  515.9 1.7 convolution_add_fusion.15
  517.6 1.3 constant_dynamic-slice_fusion.11
  524.6 2.7 fusion.146
  527.4 2.7 convolution_add_fusion.15
  530.0 1.3 constant_dynamic-slice_fusion.11
  537.0 2.7 fusion.146
  539.8 2.7 convolution_add_fusion.15
  542.4 1.3 constant_dynamic-slice_fusion.11
  549.4 2.7 fusion.146
  552.1 2.7 convolution_add_fusion.15
  554.8 1.3 constant_dynamic-slice_fusion.11
  561.8 2.7 fusion.146
  564.5 2.6 convolution_add_fusion.15
  567.2 1.3 constant_dynamic-slice_fusion.11
  574.2 2.7 fusion.146
  576.9 2.7 convolution_add_fusion.15
  579.6 1.3 constant_dynamic-slice_fusion.11
  586.5 2.7 fusion.146
  589.3 2.7 convolution_add_fusion.15
  591.9 1.3 constant_dynamic-slice_fusion.11
  598.9 2.7 fusion.146
  601.7 2.6 convolution_add_fusion.15
  607.7 1.8 convolution_bitcast_fusion.3
  609.5 1.8 convolution_bitcast_fusion.2
  611.3 1.7 convolution_bitcast_fusion.1
  613.0 1.7 fusion.40
  616.0 1.9 fusion.39
  617.9 1.6 convolution_add_fusion.6
  621.2 273.0 %all-reduce.7.cloned.1.call-done = (f32[1024,512]{0,1:T(8,128)}, f32[1024,512]{0,1:T(8,128)}, f32[1024,512]{0,1:T(8,128)}, f32[512,1024]{1,0:T(8,128)}) async-done(((f32[1024,512]{0,1:T(8,128)}, f32[1024,512]{0,1:T(8,128)}, f32[1024,512]{0,1:T(8,128)}, f32[512,1024]{1,0:T(8,128)}), (f32[1024,512]{0,1:T(8,128)}, f32[1024,512]{0,1:T(8,128)}, f32[1024,512]{0,1:T(8,128)}, ...) | async-done | bytes 8388624
  899.6 1.4 constant_dynamic-slice_fusion.4
  (352 shorter events, 129.0 us)
Async XLA Ops:
  7.2 109.9 %copy-start = (bf16[1,128,1024]{2,1,0:T(8,128)(2,1)S(1)}, bf16[1,128,1024]{2,1,0:T(8,128)(2,1)}, u32[]{:S(2)}) copy-start(bf16[1,128,1024]{2,1,0:T(8,128)(2,1)} %param.12) | copy-start | bytes 786436
  7.2 56.9 %all-gather.9.cloned.1.call-start = ((), (), s32[]{:S(2)}) async-start(), calls=%async_computation | async-start | bytes 1179648 | tf_op jit(solution)/shard_map/all_gather | solution.py:64
  7.9 109.1 %all-gather.15.cloned.1.call-start = ((), (), s32[]{:S(2)}) async-start(), calls=%async_computation.3 | async-start | bytes 1179648 | tf_op jit(solution)/shard_map/all_gather | solution.py:65
  8.7 161.3 %all-gather.13.cloned.1.call-start = ((), (), s32[]{:S(2)}) async-start(), calls=%async_computation.2 | async-start | bytes 1179648 | tf_op jit(solution)/shard_map/all_gather | solution.py:63
  9.4 213.4 %all-gather.19.cloned.1.call-start = ((), (), s32[]{:S(2)}) async-start(), calls=%async_computation.5 | async-start | bytes 1179648 | tf_op jit(solution)/shard_map/all_gather | solution.py:66
  10.0 162.4 %copy-start.19 = (s32[32,32]{1,0:T(8,128)S(1)}, s32[32,32]{1,0:T(8,128)}, u32[]{:S(2)}) copy-start(s32[32,32]{1,0:T(8,128)} %param.18) | copy-start | bytes 12292
  10.0 163.0 %copy-start.16 = (s32[64]{0:T(128)S(1)}, s32[64]{0:T(128)}, u32[]{:S(2)}) copy-start(s32[64]{0:T(128)} %param.19) | copy-start | bytes 772
  10.0 281.1 %all-gather.11.cloned.1.call-start = ((), (), s32[]{:S(2)}) async-start(), calls=%async_computation.1 | async-start | bytes 4325376 | tf_op jit(solution)/shard_map/all_gather | solution.py:116
  66.4 108.1 %copy-start.9 = (bf16[128,512]{1,0:T(8,128)(2,1)S(1)}, bf16[128,512]{1,0:T(8,128)(2,1)}, u32[]{:S(2)}) copy-start(bf16[128,512]{1,0:T(8,128)(2,1)} %convolution_convert_fusion.3) | copy-start | bytes 393220
  66.4 156.4 %copy-start.6 = (bf16[1,128,1024]{2,1,0:T(8,128)(2,1)S(1)}, bf16[1,128,1024]{2,1,0:T(8,128)(2,1)}, u32[]{:S(2)}) copy-start(bf16[1,128,1024]{2,1,0:T(8,128)(2,1)} %param.13) | copy-start | bytes 786436
  66.4 293.4 %all-gather.17.cloned.1.call-start = ((), (), s32[]{:S(2)}) async-start(), calls=%async_computation.4 | async-start | bytes 4325376 | tf_op jit(solution)/shard_map/all_gather | solution.py:117
  119.2 56.0 %copy-start.10 = (bf16[128,512]{1,0:T(8,128)(2,1)S(1)}, bf16[128,512]{1,0:T(8,128)(2,1)}, u32[]{:S(2)}) copy-start(bf16[128,512]{1,0:T(8,128)(2,1)} %convolution_convert_fusion.1) | copy-start | bytes 393220
  119.3 387.3 %all-gather.21.cloned.1.call-start = ((), (), s32[]{:S(2)}) async-start(), calls=%async_computation.6 | async-start | bytes 4325376 | tf_op jit(solution)/shard_map/all_gather | solution.py:159
  172.2 334.4 %all-gather.23.cloned.1.call-start = ((), (), s32[]{:S(2)}) async-start(), calls=%async_computation.7 | async-start | bytes 4325376 | tf_op jit(solution)/shard_map/all_gather | solution.py:162
  224.5 0.7 copy-start.8
  225.2 669.0 %all-reduce.7.cloned.1.call-start = ((), (), s32[]{:S(2)}) async-start(), calls=%async_computation.8 | async-start | bytes 16777216
  438.1 69.1 %copy-start.17 = (f32[4,128]{1,0:T(4,128)}, f32[4,128]{1,0:T(4,128)S(1)}, u32[]{:S(2)}) copy-start(f32[4,128]{1,0:T(4,128)S(1)} %get-tuple-element.746) | copy-start | bytes 6148
  438.1 69.1 %copy-start.18 = (f32[4,128]{1,0:T(4,128)}, f32[4,128]{1,0:T(4,128)S(1)}, u32[]{:S(2)}) copy-start(f32[4,128]{1,0:T(4,128)S(1)} %get-tuple-element.747) | copy-start | bytes 6148
  507.2 5.5 copy-start.15
  508.7 5.0 copy-start.1
  517.6 5.5 copy-start.15
  519.2 5.0 copy-start.1
  530.0 5.5 copy-start.15
  531.5 5.0 copy-start.1
  542.4 5.5 copy-start.15
  543.9 5.0 copy-start.1
  554.8 5.5 copy-start.15
  556.3 5.0 copy-start.1
  567.2 5.5 copy-start.15
  568.7 5.0 copy-start.1
  579.5 5.5 copy-start.15
  581.1 5.0 copy-start.1
  591.9 5.5 copy-start.15
  593.5 5.0 copy-start.1
  606.5 4.9 copy-start.11
  607.7 3.6 copy-start.14
  607.7 5.3 copy-start.13
  609.5 3.5 copy-start.7
  614.8 1.2 copy-start.5
  614.8 3.2 copy-start.4
  614.8 4.7 copy-start.2
  617.9 2.1 copy-start.3
  617.9 2.1 copy-start.12
Sparse Core Ops, SparseCore 0:
  10.7 53.4 all-gather.8
  66.8 50.2 all-gather.14
  119.7 50.2 all-gather.12
  172.5 50.2 all-gather.18
  225.0 65.9 all-gather.10
  293.4 66.4 all-gather.16
  361.7 66.6 all-gather.20
  430.3 66.8 all-gather.22
  614.9 279.2 all-reduce.6
where the time goes:
time: 910 us; the launch traced here: 908 us
  waiting for transfers between devices  612 us (67%)
  matrix products  122 us (13%)
  local copies, waits for them, and re-layouts  71.7 us (8%)
  blocking collectives  68.5 us (8%)
  between operations  14.1 us (2%)
  loops' own time  11.7 us (1%)
    unnamed x10, waiting for transfers between devices  276 us
    all_gather x1, waiting for transfers between devices, body(): lax.all_gather(values, 'ctx', axis=0, tiled=True)  68.8 us
    all_gather x1, waiting for transfers between devices, body(): lax.all_gather(keys, 'ctx', axis=0, tiled=True)  65.8 us
    all_gather x1, waiting for transfers between devices, body(): lax.all_gather(w_key, 'fsdp', axis=0, tiled=True)  54.1 us
    all_gather x1, waiting for transfers between devices, body(): lax.all_gather(w_query, 'fsdp', axis=0, tiled=True)  50.7 us
    all_gather x1, waiting for transfers between devices, body(): lax.all_gather(w_value, 'fsdp', axis=0, tiled=True)  50.6 us
    dynamic_slice x64, local copies, waits for them, and re-layouts, over_blocks(): carry, _ = lax.scan(scan_step, carry, (numbers, stacked))  47.6 us
    all_gather x1, waiting for transfers between devices, body(): lax.all_gather(w_out, 'fsdp', axis=0, tiled=True)  46.9 us
  transfers between devices with their start and end apart: 9, of which 7 were waited for; matrix products, arithmetic and copies ran while one was open for 10% of the time, Pallas kernels for 0%

commit v1 on v0

--- a/solution.py
+++ b/solution.py
@@ -10,6 +10,11 @@
 SPAN = 64
 NEG = -1e30
 HIGH = lax.Precision.HIGHEST
+
+
+def exchange_gather(x, mesh_axis, d):
+    outgoing = jnp.stack([x] * lax.axis_size(mesh_axis))
+    return jnp.concatenate(lax.all_to_all(outgoing, mesh_axis, 0, 0), axis=d)
 
 
 def block_ids(span_order, start, count):
@@ -112,10 +117,7 @@
     top, total, out_acc, mix_acc, key_acc, dot_acc = over_blocks(
         sweep_keys,
         begin,
-        (
-            lax.all_gather(keys, "ctx", axis=0, tiled=True),
-            lax.all_gather(values, "ctx", axis=0, tiled=True),
-        ),
+        (lax.all_gather(keys, "ctx", axis=0, tiled=True), exchange_gather(values, "ctx", 0)),
     )
     share = 1.0 / total
     combined = out_acc * share[:, :, None]

time: 910 us -> 865 us (0.951)
  waiting for transfers between devices: 612 us -> 557 us
    all_gather x1 -> x0, waiting for transfers between devices: 68.8 us -> none  [body(): lax.all_gather(values, 'ctx', axis=0, tiled=True)]
    all_gather x1, waiting for transfers between devices: 65.8 us -> 79.6 us  [body(): lax.all_gather(keys, 'ctx', axis=0, tiled=True)]
    unnamed x10 -> x9, waiting for transfers between devices: 276 us -> 275 us
  transfers between devices with their start and end apart: 9 -> 9, of which waited for: 7 -> 6; matrix products, arithmetic and copies ran while one was open for 10% -> 11% of each run, Pallas kernels for 0% -> 0%
where the time goes in v1:
time: 865 us; the launch traced here: 863 us
  waiting for transfers between devices  557 us (64%)
  matrix products  122 us (14%)
  local copies, waits for them, and re-layouts  74 us (9%)
  blocking collectives  67.3 us (8%)
  between operations  14.4 us (2%)
  loops' own time  12.1 us (1%)
  starting transfers between devices  9.15 us (1%)
    unnamed x9, waiting for transfers between devices  275 us
    all_gather x1, waiting for transfers between devices, body(): lax.all_gather(keys, 'ctx', axis=0, tiled=True)  79.6 us
    all_gather x1, waiting for transfers between devices, body(): lax.all_gather(w_key, 'fsdp', axis=0, tiled=True)  54.1 us
    all_gather x1, waiting for transfers between devices, body(): lax.all_gather(w_value, 'fsdp', axis=0, tiled=True)  50.7 us
    all_gather x1, waiting for transfers between devices, body(): lax.all_gather(w_query, 'fsdp', axis=0, tiled=True)  50.6 us
    dynamic_slice x64, local copies, waits for them, and re-layouts, over_blocks(): carry, _ = lax.scan(scan_step, carry, (numbers, stacked))  48 us
    all_gather x1, waiting for transfers between devices, body(): lax.all_gather(w_out, 'fsdp', axis=0, tiled=True)  46.5 us
    all_gather x1, blocking collectives, body(): lax.all_gather(delta_rows, 'ctx', axis=0, tiled=True)  33.8 us
  transfers between devices with their start and end apart: 9, of which 6 were waited for; matrix products, arithmetic and copies ran while one was open for 11% of the time, Pallas kernels for 0%

profile of v1, /device:TPU:2, one launch (start us, length us, event | category | flops | bytes accessed | tf_op | source)
XLA Modules:
  0.0 862.6 jit_solution(12292728135193235116)
XLA Ops:
  10.0 54.1 %all-gather.8.cloned.1.call-done = bf16[1024,512]{1,0:T(8,128)(2,1)} async-done(((bf16[128,512]{1,0:T(8,128)(2,1)}), bf16[1024,512]{1,0:T(8,128)(2,1)}) %all-gather.8.cloned.1.call-update) | async-done | bytes 1048592 | tf_op jit(solution)/shard_map/all_gather | solution.py:69
  64.1 2.3 convolution_convert_fusion.3
  66.5 50.6 %all-gather.12.cloned.1.call-done = bf16[1024,512]{1,0:T(8,128)(2,1)} async-done(((bf16[128,512]{1,0:T(8,128)(2,1)}), bf16[1024,512]{1,0:T(8,128)(2,1)}) %all-gather.12.cloned.1.call-update) | async-done | bytes 1048592 | tf_op jit(solution)/shard_map/all_gather | solution.py:68
  117.1 2.2 convolution_convert_fusion.2
  119.3 50.7 %all-gather.14.cloned.1.call-done = bf16[1024,512]{1,0:T(8,128)(2,1)} async-done(((bf16[128,512]{1,0:T(8,128)(2,1)}), bf16[1024,512]{1,0:T(8,128)(2,1)}) %all-gather.14.cloned.1.call-update) | async-done | bytes 1048592 | tf_op jit(solution)/shard_map/all_gather | solution.py:70
  170.0 1.5 convolution_convert_fusion.1
  171.5 2.4 stack.2
  174.0 8.8 %all-to-all-start = ((bf16[32,128,512]{2,1,0:T(8,128)(2,1)}), bf16[32,128,512]{2,1,0:T(8,128)(2,1)}, u32[]{:S(2)}, u32[]{:S(2)}) async-start(bf16[32,128,512]{2,1,0:T(8,128)(2,1)} %stack.2), calls=%async_computation | async-start | bytes 8388608 | tf_op jit(solution)/shard_map/all_to_all | solution.py:17
  184.2 46.5 %all-gather.16.cloned.1.call-done = bf16[512,1024]{1,0:T(8,128)(2,1)} async-done(((bf16[64,1024]{1,0:T(8,128)(2,1)}), bf16[512,1024]{1,0:T(8,128)(2,1)}) %all-gather.16.cloned.1.call-update) | async-done | bytes 1048592 | tf_op jit(solution)/shard_map/all_gather | solution.py:71
  230.7 2.4 convolution_convert_fusion
  235.5 79.6 %all-gather.10.cloned.1.call-done = bf16[4096,512]{1,0:T(8,128)(2,1)} async-done(((bf16[128,512]{1,0:T(8,128)(2,1)}), bf16[4096,512]{1,0:T(8,128)(2,1)}) %all-gather.10.cloned.1.call-update) | async-done | bytes 4194320 | tf_op jit(solution)/shard_map/all_gather | solution.py:120
  315.6 75.2 %while.40 = (s32[]{:T(128)}, f32[4,128]{1,0:T(4,128)S(1)}, f32[4,128]{1,0:T(4,128)S(1)}, f32[4,128,128]{2,1,0:T(8,128)S(1)}, f32[4,128,128]{2,1,0:T(8,128)S(1)},...) while((s32[]{:T(128)}, f32[4,128]{1,0:T(4,128)S(1)}, ...), condition=%wide.region_6.7_spmd.clone, body=%wide.region_1.6_spmd.clone.sunk | while | flops 1351104000 | bytes 16581600 | solution.py:46
  393.3 33.5 %all_gather.33 = f32[4096,4]{0,1:T(4,128)} all-gather(f32[128,4]{0,1:T(4,128)S(1)} %get-tuple-element.792), channel_id=1, replica_groups=mesh['fsdp'=8,'ctx'=32] {'ctx'}, dimensions={0}, use_global_device_ids=true | all-gather | bytes 67584 | tf_op jit(solution)/shard_map/all_gather | solution.py:167
  426.8 33.8 %all_gather.35 = f32[4096,4]{0,1:T(4,128)} all-gather(f32[128,4]{0,1:T(4,128)S(1)} %bitcast.203), channel_id=1, replica_groups=mesh['fsdp'=8,'ctx'=32] {'ctx'}, dimensions={0}, use_global_device_ids=true | all-gather | bytes 67584 | tf_op jit(solution)/shard_map/all_gather | solution.py:168
  461.2 98.1 %while.41 = (s32[]{:T(128)}, f32[4,128,128]{2,1,0:T(8,128)}, f32[4,128,128]{2,1,0:T(8,128)}, s32[8]{0:T(128)}, s32[64]{0:T(128)S(1)}, /*index=5*/bf16[32,32]{1,0...) while((s32[]{:T(128)}, f32[4,128,128]{2,1,0:T(8,128)}, ...), condition=%wide.region_9.10_spmd.clone, body=%wide.region_7.9_spmd.clone.sunk | while | flops 946874368 | bytes 14089224 | solution.py:46
  461.2 1.3 constant_dynamic-slice_fusion.11
  463.5 1.3 dynamic_slice.82
  468.3 1.8 fusion.146
  470.1 1.7 convolution_add_fusion.15
  474.1 1.3 dynamic_slice.82
  478.9 2.7 fusion.146
  481.6 2.7 convolution_add_fusion.15
  486.6 1.3 dynamic_slice.82
  491.4 2.7 fusion.146
  494.1 2.7 convolution_add_fusion.15
  499.1 1.3 dynamic_slice.82
  503.9 2.7 fusion.146
  506.6 2.7 convolution_add_fusion.15
  511.6 1.3 dynamic_slice.82
  516.4 2.7 fusion.146
  519.1 2.7 convolution_add_fusion.15
  524.1 1.3 dynamic_slice.82
  528.9 2.7 fusion.146
  531.6 2.7 convolution_add_fusion.15
  536.6 1.3 dynamic_slice.82
  541.4 2.7 fusion.146
  544.1 2.7 convolution_add_fusion.15
  549.1 1.3 dynamic_slice.82
  553.9 2.7 fusion.146
  556.6 2.7 convolution_add_fusion.15
  562.7 1.8 convolution_bitcast_fusion.3
  564.5 1.8 convolution_bitcast_fusion.2
  566.3 1.7 convolution_bitcast_fusion.1
  568.0 1.7 fusion.40
  570.9 1.9 fusion.39
  572.9 1.6 convolution_add_fusion.6
  576.2 272.8 %all-reduce.7.cloned.1.call-done = (f32[1024,512]{0,1:T(8,128)}, f32[1024,512]{0,1:T(8,128)}, f32[1024,512]{0,1:T(8,128)}, f32[512,1024]{1,0:T(8,128)}) async-done(((f32[1024,512]{0,1:T(8,128)}, f32[1024,512]{0,1:T(8,128)}, f32[1024,512]{0,1:T(8,128)}, f32[512,1024]{1,0:T(8,128)}), (f32[1024,512]{0,1:T(8,128)}, f32[1024,512]{0,1:T(8,128)}, f32[1024,512]{0,1:T(8,128)}, ...) | async-done | bytes 8388624
  854.4 1.4 constant_dynamic-slice_fusion.4
  (350 shorter events, 129.8 us)
Async XLA Ops:
  7.2 109.9 %copy-start = (bf16[1,128,1024]{2,1,0:T(8,128)(2,1)S(1)}, bf16[1,128,1024]{2,1,0:T(8,128)(2,1)}, u32[]{:S(2)}) copy-start(bf16[1,128,1024]{2,1,0:T(8,128)(2,1)} %param.12) | copy-start | bytes 786436
  7.2 56.9 %all-gather.8.cloned.1.call-start = ((), (), s32[]{:S(2)}) async-start(), calls=%async_computation.1 | async-start | bytes 1179648 | tf_op jit(solution)/shard_map/all_gather | solution.py:69
  7.9 109.1 %all-gather.12.cloned.1.call-start = ((), (), s32[]{:S(2)}) async-start(), calls=%async_computation.3 | async-start | bytes 1179648 | tf_op jit(solution)/shard_map/all_gather | solution.py:68
  8.7 161.3 %all-gather.14.cloned.1.call-start = ((), (), s32[]{:S(2)}) async-start(), calls=%async_computation.4 | async-start | bytes 1179648 | tf_op jit(solution)/shard_map/all_gather | solution.py:70
  9.4 221.3 %all-gather.16.cloned.1.call-start = ((), (), s32[]{:S(2)}) async-start(), calls=%async_computation.5 | async-start | bytes 1179648 | tf_op jit(solution)/shard_map/all_gather | solution.py:71
  10.0 305.1 %all-gather.10.cloned.1.call-start = ((), (), s32[]{:S(2)}) async-start(), calls=%async_computation.2 | async-start | bytes 4325376 | tf_op jit(solution)/shard_map/all_gather | solution.py:120
  66.4 394.2 %all-gather.18.cloned.1.call-start = ((), (), s32[]{:S(2)}) async-start(), calls=%async_computation.6 | async-start | bytes 4325376 | tf_op jit(solution)/shard_map/all_gather | solution.py:161
  174.0 9.0 %copy-start.18 = (s32[32,32]{1,0:T(8,128)S(1)}, s32[32,32]{1,0:T(8,128)}, u32[]{:S(2)}) copy-start(s32[32,32]{1,0:T(8,128)} %param.18) | copy-start | bytes 12292
  174.0 9.6 %copy-start.15 = (s32[64]{0:T(128)S(1)}, s32[64]{0:T(128)}, u32[]{:S(2)}) copy-start(s32[64]{0:T(128)} %param.19) | copy-start | bytes 772
  174.0 56.7 %copy-start.6 = (bf16[1,128,1024]{2,1,0:T(8,128)(2,1)S(1)}, bf16[1,128,1024]{2,1,0:T(8,128)(2,1)}, u32[]{:S(2)}) copy-start(bf16[1,128,1024]{2,1,0:T(8,128)(2,1)} %param.13) | copy-start | bytes 786436
  174.0 59.2 %copy-start.8 = (bf16[128,512]{1,0:T(8,128)(2,1)S(1)}, bf16[128,512]{1,0:T(8,128)(2,1)}, u32[]{:S(2)}) copy-start(bf16[128,512]{1,0:T(8,128)(2,1)} %convolution_convert_fusion.2) | copy-start | bytes 393220
  174.0 141.1 %all-to-all-start = ((bf16[32,128,512]{2,1,0:T(8,128)(2,1)}), bf16[32,128,512]{2,1,0:T(8,128)(2,1)}, u32[]{:S(2)}, u32[]{:S(2)}) async-start(bf16[32,128,512]{2,1,0:T(8,128)(2,1)} %stack.2), calls=%async_computation | async-start | bytes 8388608 | tf_op jit(solution)/shard_map/all_to_all | solution.py:17
  182.8 51.3 %copy-start.9 = (bf16[128,512]{1,0:T(8,128)(2,1)S(1)}, bf16[128,512]{1,0:T(8,128)(2,1)}, u32[]{:S(2)}) copy-start(bf16[128,512]{1,0:T(8,128)(2,1)} %convolution_convert_fusion.3) | copy-start | bytes 393220
  182.8 277.8 %all-gather.20.cloned.1.call-start = ((), (), s32[]{:S(2)}) async-start(), calls=%async_computation.7 | async-start | bytes 4325376 | tf_op jit(solution)/shard_map/all_gather | solution.py:164
  233.1 615.9 %all-reduce.7.cloned.1.call-start = ((), (), s32[]{:S(2)}) async-start(), calls=%async_computation.8 | async-start | bytes 16777216
  393.3 67.9 %copy-start.16 = (f32[4,128]{1,0:T(4,128)}, f32[4,128]{1,0:T(4,128)S(1)}, u32[]{:S(2)}) copy-start(f32[4,128]{1,0:T(4,128)S(1)} %get-tuple-element.780) | copy-start | bytes 6148
  393.3 67.9 %copy-start.17 = (f32[4,128]{1,0:T(4,128)}, f32[4,128]{1,0:T(4,128)S(1)}, u32[]{:S(2)}) copy-start(f32[4,128]{1,0:T(4,128)S(1)} %get-tuple-element.781) | copy-start | bytes 6148
  461.2 5.6 copy-start.14
  462.7 5.1 copy-start.1
  471.8 5.6 copy-start.14
  473.3 5.1 copy-start.1
  484.3 5.6 copy-start.14
  485.8 5.1 copy-start.1
  496.8 5.6 copy-start.14
  498.3 5.1 copy-start.1
  509.3 5.6 copy-start.14
  510.8 5.1 copy-start.1
  521.8 5.6 copy-start.14
  523.3 5.1 copy-start.1
  534.3 5.6 copy-start.14
  535.8 5.1 copy-start.1
  546.8 5.6 copy-start.14
  548.3 5.1 copy-start.1
  561.4 4.9 copy-start.10
  562.6 3.6 copy-start.13
  562.6 5.3 copy-start.12
  564.5 3.5 copy-start.7
  569.7 1.2 copy-start.5
  569.7 3.2 copy-start.3
  569.7 4.7 copy-start.2
  572.9 2.1 copy-start.4
  572.9 2.1 copy-start.11
Sparse Core Ops, SparseCore 0:
  10.7 53.4 all-gather.7
  66.8 50.2 all-gather.11
  119.7 50.2 all-gather.13
  172.5 58.1 all-gather.15
  233.0 82.0 all-gather.9
  316.8 64.7 all-gather.17
  383.4 66.4 all-gather.19
  569.9 279.0 all-reduce.6
